TPU v7x, 256 devices: a whole 4x4x8 slice. The times are simulated.
256 devices in a mesh: gx: 16 (over z, core), gy: 16 (over y, x).
Axes of the slice: x: 4, y: 4, z: 8, core: 2. Of those that a mesh axis runs over, the one named last changes fastest.
Arguments:
- latent_noise: float32 [1024, 65536], P('gx', 'gy'), may hold values from -6 to 6
- kappa_sq: float32 [1024, 1024], P('gx', 'gy'), may hold values from 0.25 to 4
- obs_cell: int32 [65536], P(('gx', 'gy')), may hold values from 0 to 4095
- obs_value: float32 [65536], P(('gx', 'gy')), may hold values from -6 to 6
- obs_var: float32 [65536], P(('gx', 'gy')), may hold values from 0.1 to 1
Outputs:
- latent_new: float32 [1024, 65536], P('gx', 'gy')
- prior_field: float32 [1024, 65536], P('gx', 'gy')
Inputs may be any that keep to these rules, and one draw needn't show every extreme that they name: obs_cell[j] is a cell of the block held by device j // 256 in the order of gx+gy (gx slowest), written as row * 64 + column within that block.
All inputs are finite; a program needn't handle non-finite values.
Results may differ from a plain program's by a relative error of at most 0.0001.
Values sent between devices are 32-bit elements; how exact they have to be, the bound alone decides.
No kernel may reach another device: no remote copies, remote signals or barrier semaphores. Data moves between devices by JAX's collectives and lax.ppermute only.
A program may use at most 64 MiB of HBM per device.

v0:
```python
import jax
import jax.numpy as jnp
import numpy as np
from jax import lax
from jax.sharding import PartitionSpec as P

MEMBERS = 64
SWEEPS = 4
LOWER_EDGE = 0.25
UPPER_EDGE = 12.0


def padded(block, sides, width):
    for axis, dim in sides:
        count = lax.axis_size(axis)
        forward = [(i, i + 1) for i in range(count - 1)]
        backward = [(target, source) for source, target in forward]
        low = lax.ppermute(
            lax.slice_in_dim(block, block.shape[dim] - width, None, axis=dim), axis, forward
        )
        high = lax.ppermute(lax.slice_in_dim(block, 0, width, axis=dim), axis, backward)
        block = jnp.concatenate([low, block, high], axis=dim)
    return block


def cheb_coeffs(terms):
    angles = np.pi * (np.arange(64) + 0.5) / 64.0
    nodes = 0.5 * (UPPER_EDGE + LOWER_EDGE) + 0.5 * (UPPER_EDGE - LOWER_EDGE) * np.cos(angles)
    values = []
    for order in range(terms):
        coeff = 2.0 / 64.0 * np.sum(np.cos(order * angles) / nodes)
        if order == 0:
            coeff = 0.5 * coeff
        values.append(float(coeff))
    return values


def chol_solve(factor, rhs):
    lower_sol = lax.linalg.triangular_solve(factor, rhs, left_side=True, lower=True)
    return lax.linalg.triangular_solve(
        factor, lower_sol, left_side=True, lower=True, transpose_a=True
    )


def stencil(field, along_x, along_y, diagonal):
    beside = along_x[2:] + along_x[:-2] + along_y[:, 2 * MEMBERS :] + along_y[:, : -2 * MEMBERS]
    applied = diagonal * field - beside
    return (2.0 * applied - (UPPER_EDGE + LOWER_EDGE) * field) / (UPPER_EDGE - LOWER_EDGE)


def chebyshev(start, scaled, coeffs):
    earlier = start
    current = scaled(start)
    total = coeffs[0] * start + coeffs[1] * current
    for order in range(2, len(coeffs)):
        following = 2.0 * scaled(current) - earlier
        total = total + coeffs[order] * following
        earlier, current = (current, following)
    return total


def per_device(latent_noise, kappa_sq, obs_cell, obs_value, obs_var):
    rows_x, width = latent_noise.shape
    cells_y = width // MEMBERS
    coeffs = cheb_coeffs(SWEEPS + 1)
    diagonal = jnp.repeat(kappa_sq + 4.0, MEMBERS, axis=1)

    def scaled(field):
        along_x = padded(field, (("gx", 0),), 1)
        along_y = padded(field, (("gy", 1),), MEMBERS)
        return stencil(field, along_x, along_y, diagonal)

    prior_field = chebyshev(latent_noise, scaled, coeffs)
    field_cells = prior_field.reshape(rows_x * cells_y, MEMBERS)
    predicted = jnp.take(field_cells, obs_cell, axis=0)
    weight = 1.0 / obs_var
    misfits = obs_value[:, None] - predicted
    own_misfit = jnp.sum(misfits * misfits * weight[:, None])
    spread = predicted - jnp.mean(predicted, axis=1, keepdims=True)
    scale_down = float(MEMBERS * (MEMBERS - 1))
    misfit_total = lax.psum(own_misfit, ("gx", "gy"))
    inflation = 1.0 + misfit_total / scale_down
    scaled_spread = spread * (weight / inflation)[:, None]
    own_gram = jnp.dot(
        scaled_spread.T, spread, precision=lax.Precision.HIGHEST, preferred_element_type=jnp.float32
    )
    own_cross = jnp.dot(
        scaled_spread.T,
        misfits,
        precision=lax.Precision.HIGHEST,
        preferred_element_type=jnp.float32,
    )
    gram, cross = lax.psum((own_gram, own_cross), ("gx", "gy"))
    system = (MEMBERS - 1) * jnp.eye(MEMBERS, dtype=jnp.float32) + gram
    factor = jnp.linalg.cholesky(system)
    gain = chol_solve(factor, cross)
    latent_cells = latent_noise.reshape(rows_x * cells_y, MEMBERS)
    deviation = latent_cells - jnp.mean(latent_cells, axis=1, keepdims=True)
    update = jnp.dot(
        deviation, gain, precision=lax.Precision.HIGHEST, preferred_element_type=jnp.float32
    )
    latent_new = (latent_cells + update).reshape(rows_x, width)
    return (latent_new, prior_field)


def solution(mesh):
    placed = (P("gx", "gy"), P("gx", "gy"), P(("gx", "gy")), P(("gx", "gy")), P(("gx", "gy")))
    return jax.shard_map(
        per_device,
        mesh=mesh,
        in_specs=placed,
        out_specs=(P("gx", "gy"), P("gx", "gy")),
        check_vma=False,
    )
```

profile of v0, /device:TPU:1, one launch (start us, length us, event | category | flops | bytes accessed | tf_op | source)
XLA Modules:
  0.0 266.3 jit_solution(12779640378611144372)
XLA Ops:
  2.8 4.6 %collective-permute-start.3 = (f32[64,64]{1,0:T(8,128)S(1)}, f32[64,64]{1,0:T(8,128)S(1)}, u32[]{:S(2)}, u32[]{:S(2)}) collective-permute-start(f32[64,64]{1,0:T(8,128)S(1)} %get-tuple-element.21), channel_id=1, source_target_pairs={{0,1},{1,2},{2,3},{3,4},{4,5},{5,6},{6,7},{7,8},{8,9},{9,10},{10,1... | collective-permute-start | bytes 49160 | tf_op jit(solution)/shard_map/ppermute | solution.py:18
  8.4 5.1 %collective-permute-start = (f32[1,4096]{1,0:T(1,128)S(1)}, f32[1,4096]{1,0:T(1,128)S(1)}, u32[]{:S(2)}, u32[]{:S(2)}) collective-permute-start(f32[1,4096]{1,0:T(1,128)S(1)} %get-tuple-element.18), channel_id=1, source_target_pairs={{16,0},{32,16},{48,32},{64,48},{80,64},{96,80},{112,96},{128,112},... | collective-permute-start | bytes 49160 | tf_op jit(solution)/shard_map/ppermute | solution.py:21
  15.4 2.0 reshape.43
  18.1 1.9 broadcast_in_dim.23
  20.1 3.0 %reshape.44 = f32[64,4096]{1,0:T(8,128)} reshape(f32[64,64,64]{2,1,0:T(8,128)} %broadcast_in_dim.23) | data formatting | bytes 2097152 | tf_op jit(solution)/shard_map/reshape | solution.py:66
  23.1 1.9 broadcast_multiply_fusion
  26.4 4.0 %collective-permute-start.7 = (f32[64,64]{1,0:T(8,128)S(1)}, f32[64,64]{1,0:T(8,128)S(1)}, u32[]{:S(2)}, u32[]{:S(2)}) collective-permute-start(f32[64,64]{1,0:T(8,128)S(1)} %get-tuple-element.17), channel_id=1, source_target_pairs={{0,1},{1,2},{2,3},{3,4},{4,5},{5,6},{6,7},{7,8},{8,9},{9,10},{10,1... | collective-permute-start | bytes 49160 | tf_op jit(solution)/shard_map/ppermute | solution.py:18
  30.4 3.0 %collective-permute-start.4 = (f32[1,4096]{1,0:T(1,128)S(1)}, f32[1,4096]{1,0:T(1,128)S(1)}, u32[]{:S(2)}, u32[]{:S(2)}) collective-permute-start(f32[1,4096]{1,0:T(1,128)S(1)} %get-tuple-element.14), channel_id=1, source_target_pairs={{16,0},{32,16},{48,32},{64,48},{80,64},{96,80},{112,96},{128,112},... | collective-permute-start | bytes 49160 | tf_op jit(solution)/shard_map/ppermute | solution.py:21
  33.4 2.6 collective-permute-start.5
  36.9 2.0 fusion.24
  40.3 4.0 %collective-permute-start.11 = (f32[64,64]{1,0:T(8,128)S(1)}, f32[64,64]{1,0:T(8,128)S(1)}, u32[]{:S(2)}, u32[]{:S(2)}) collective-permute-start(f32[64,64]{1,0:T(8,128)S(1)} %get-tuple-element.13), channel_id=1, source_target_pairs={{0,1},{1,2},{2,3},{3,4},{4,5},{5,6},{6,7},{7,8},{8,9},{9,10},{10,1... | collective-permute-start | bytes 49160 | tf_op jit(solution)/shard_map/ppermute | solution.py:18
  44.3 2.3 collective-permute-start.8
  46.5 4.4 %collective-permute-start.9 = (f32[1,4096]{1,0:T(1,128)S(1)}, f32[1,4096]{1,0:T(1,128)S(1)}, u32[]{:S(2)}, u32[]{:S(2)}) collective-permute-start(f32[1,4096]{1,0:T(1,128)S(1)} %get-tuple-element.11), channel_id=1, source_target_pairs={{0,16},{16,32},{32,48},{48,64},{64,80},{80,96},{96,112},{112,128},... | collective-permute-start | bytes 49160 | tf_op jit(solution)/shard_map/ppermute | solution.py:18
  51.8 2.0 fusion.16
  56.1 4.6 %collective-permute-start.15 = (f32[64,64]{1,0:T(8,128)S(1)}, f32[64,64]{1,0:T(8,128)S(1)}, u32[]{:S(2)}, u32[]{:S(2)}) collective-permute-start(f32[64,64]{1,0:T(8,128)S(1)} %get-tuple-element.9), channel_id=1, source_target_pairs={{0,1},{1,2},{2,3},{3,4},{4,5},{5,6},{6,7},{7,8},{8,9},{9,10},{10,1... | collective-permute-start | bytes 49160 | tf_op jit(solution)/shard_map/ppermute | solution.py:18
  62.6 4.5 %collective-permute-start.13 = (f32[1,4096]{1,0:T(1,128)S(1)}, f32[1,4096]{1,0:T(1,128)S(1)}, u32[]{:S(2)}, u32[]{:S(2)}) collective-permute-start(f32[1,4096]{1,0:T(1,128)S(1)} %get-tuple-element.7), channel_id=1, source_target_pairs={{0,16},{16,32},{32,48},{48,64},{64,80},{80,96},{96,112},{112,128},... | collective-permute-start | bytes 49160 | tf_op jit(solution)/shard_map/ppermute | solution.py:18
  68.7 5.6 %fusion.8 = f32[64,4096]{1,0:T(8,128)} fusion(f32[64,4096]{1,0:T(8,128)} %copy-done.2, f32[64,4096]{1,0:T(8,128)} %copy-done.3, f32[64,64]{1,0:T(8,128)S(1)} %collective-permute-done.15, f32[64,64]{1,0:T(8,128)S(1)} %collective-permute-done.14, f32[1,4096]{1,0:T(1,128)S(1)} %collective-permute-done.13, f32[1,4096]{1,0:T(1,128)S(1)} %collective-permute-done.12, ...), kind=kLoop, calls=%fused_computation.11 | loop fusion | flops 9175040 | bytes 5373952 | tf_op jit(solution)/shard_map/add | solution.py:57
  74.4 3.2 %reshape.45 = f32[4096,64]{1,0:T(8,128)} reshape(f32[64,4096]{1,0:T(8,128)} %fusion.8) | data formatting | bytes 2097152 | tf_op jit(solution)/shard_map/reshape | solution.py:74
  77.6 2.3 gather_fusion
  80.7 89.7 %psum.21 = f32[]{:T(128)} all-reduce(f32[]{:T(128)} %get-tuple-element.3), channel_id=1, replica_groups=mesh['gx'=16,'gy'=16] {'gx','gy'}, use_global_device_ids=true, to_apply=%region_3.4 | all-reduce | flops 1 | bytes 8 | tf_op jit(solution)/shard_map/psum | solution.py:81
  172.3 74.2 %all-reduce = (f32[64,64]{1,0:T(8,128)S(1)}, f32[64,64]{1,0:T(8,128)S(1)}) all-reduce(f32[64,64]{1,0:T(8,128)S(1)} %fusion.34, f32[64,64]{1,0:T(8,128)S(1)} %fusion.36), channel_id=1, replica_groups=mesh['gx'=16,'gy'=16] {'gx','gy'}, use_global_device_ids=true, to_apply=%region_7.8 | all-reduce | flops 8192 | bytes 65536 | tf_op jit(solution)/shard_map/psum | solution.py:93
  246.5 5.8 %cholesky.16 = f32[64,64]{1,0:T(8,128)S(1)} custom-call(f32[64,64]{1,0:T(8,128)S(1)} %fusion.57), custom_call_target="Cholesky" | custom-call | tf_op jit(solution)/shard_map/jit(cholesky)/cholesky | solution.py:95
  253.7 4.9 %custom-call.8 = f32[1,64,64]{1,2,0:T(8,128)S(1)} custom-call(f32[1,64,64]{2,1,0:T(8,128)S(1)} %fusion.52), custom_call_target="InvertDiagBlocksLowerTriangular" | custom-call | tf_op jit(solution)/shard_map/triangular_solve | solution.py:40
  259.1 3.7 %convolution_add_fusion = f32[4096,64]{0,1:T(8,128)} fusion(f32[4096,64]{0,1:T(8,128)S(1)} %copy-done.4, f32[64,64]{1,0:T(8,128)S(1)} %fusion.53, f32[4096,64]{1,0:T(8,128)S(1)} %reshape.43, f32[4096]{0:T(1024)S(1)} %broadcast_multiply_fusion.1), kind=kOutput, calls=%fused_computation.1 | convolution fusion | flops 201850880 | bytes 3178496 | tf_op jit(solution)/shard_map/dot_general | solution.py:99
  (71 shorter events, 23.2 us)
Async XLA Ops:
  0.6 16.8 %copy-start.5 = (f32[64,64]{1,0:T(8,128)S(1)}, f32[64,64]{1,0:T(8,128)}, u32[]{:S(2)}) copy-start(f32[64,64]{1,0:T(8,128)} %param.6) | copy-start | bytes 49156
  1.5 21.5 %collective-permute-start.2 = (f32[64,64]{1,0:T(8,128)S(1)}, f32[64,64]{1,0:T(8,128)S(1)}, u32[]{:S(2)}, u32[]{:S(2)}) collective-permute-start(f32[64,64]{1,0:T(8,128)S(1)} %get-tuple-element.20), channel_id=1, source_target_pairs={{1,0},{2,1},{3,2},{4,3},{5,4},{6,5},{7,6},{8,7},{9,8},{10,9},{11,1... | collective-permute-start | bytes 49160 | tf_op jit(solution)/shard_map/ppermute | solution.py:21
  2.8 20.3 %collective-permute-start.3 = (f32[64,64]{1,0:T(8,128)S(1)}, f32[64,64]{1,0:T(8,128)S(1)}, u32[]{:S(2)}, u32[]{:S(2)}) collective-permute-start(f32[64,64]{1,0:T(8,128)S(1)} %get-tuple-element.21), channel_id=1, source_target_pairs={{0,1},{1,2},{2,3},{3,4},{4,5},{5,6},{6,7},{7,8},{8,9},{9,10},{10,1... | collective-permute-start | bytes 49160 | tf_op jit(solution)/shard_map/ppermute | solution.py:18
  8.4 14.7 %collective-permute-start = (f32[1,4096]{1,0:T(1,128)S(1)}, f32[1,4096]{1,0:T(1,128)S(1)}, u32[]{:S(2)}, u32[]{:S(2)}) collective-permute-start(f32[1,4096]{1,0:T(1,128)S(1)} %get-tuple-element.18), channel_id=1, source_target_pairs={{16,0},{32,16},{48,32},{64,48},{80,64},{96,80},{112,96},{128,112},... | collective-permute-start | bytes 49160 | tf_op jit(solution)/shard_map/ppermute | solution.py:21
  13.5 4.6 %copy-start.8 = (s32[256]{0:T(256)S(1)}, s32[256]{0:T(256)}, u32[]{:S(2)}) copy-start(s32[256]{0:T(256)} %param.7) | copy-start | bytes 3076
  13.5 9.6 %collective-permute-start.1 = (f32[1,4096]{1,0:T(1,128)S(1)}, f32[1,4096]{1,0:T(1,128)S(1)}, u32[]{:S(2)}, u32[]{:S(2)}) collective-permute-start(f32[1,4096]{1,0:T(1,128)S(1)} %get-tuple-element.19), channel_id=1, source_target_pairs={{0,16},{16,32},{32,48},{48,64},{64,80},{80,96},{96,112},{112,128},... | collective-permute-start | bytes 49160 | tf_op jit(solution)/shard_map/ppermute | solution.py:18
  20.1 3.0 %copy-start = (f32[64,4096]{1,0:T(8,128)S(1)}, f32[64,4096]{1,0:T(8,128)}, u32[]{:S(2)}) copy-start(f32[64,4096]{1,0:T(8,128)} %param.5) | copy-start | bytes 3145732
  23.0 13.0 %copy-start.6 = (f32[256]{0:T(256)S(1)}, f32[256]{0:T(256)}, u32[]{:S(2)}) copy-start(f32[256]{0:T(256)} %param.9) | copy-start | bytes 3076
  23.0 13.8 %copy-start.1 = (f32[64,4096]{1,0:T(8,128)S(1)}, f32[64,4096]{1,0:T(8,128)}, u32[]{:S(2)}) copy-start(f32[64,4096]{1,0:T(8,128)} %reshape.44) | copy-start | bytes 3145732
  25.1 10.9 %collective-permute-start.6 = (f32[64,64]{1,0:T(8,128)S(1)}, f32[64,64]{1,0:T(8,128)S(1)}, u32[]{:S(2)}, u32[]{:S(2)}) collective-permute-start(f32[64,64]{1,0:T(8,128)S(1)} %get-tuple-element.16), channel_id=1, source_target_pairs={{1,0},{2,1},{3,2},{4,3},{5,4},{6,5},{7,6},{8,7},{9,8},{10,9},{11,1... | collective-permute-start | bytes 49160 | tf_op jit(solution)/shard_map/ppermute | solution.py:21
  26.4 9.6 %collective-permute-start.7 = (f32[64,64]{1,0:T(8,128)S(1)}, f32[64,64]{1,0:T(8,128)S(1)}, u32[]{:S(2)}, u32[]{:S(2)}) collective-permute-start(f32[64,64]{1,0:T(8,128)S(1)} %get-tuple-element.17), channel_id=1, source_target_pairs={{0,1},{1,2},{2,3},{3,4},{4,5},{5,6},{6,7},{7,8},{8,9},{9,10},{10,1... | collective-permute-start | bytes 49160 | tf_op jit(solution)/shard_map/ppermute | solution.py:18
  30.4 5.6 %collective-permute-start.4 = (f32[1,4096]{1,0:T(1,128)S(1)}, f32[1,4096]{1,0:T(1,128)S(1)}, u32[]{:S(2)}, u32[]{:S(2)}) collective-permute-start(f32[1,4096]{1,0:T(1,128)S(1)} %get-tuple-element.14), channel_id=1, source_target_pairs={{16,0},{32,16},{48,32},{64,48},{80,64},{96,80},{112,96},{128,112},... | collective-permute-start | bytes 49160 | tf_op jit(solution)/shard_map/ppermute | solution.py:21
  33.4 3.5 %collective-permute-start.5 = (f32[1,4096]{1,0:T(1,128)S(1)}, f32[1,4096]{1,0:T(1,128)S(1)}, u32[]{:S(2)}, u32[]{:S(2)}) collective-permute-start(f32[1,4096]{1,0:T(1,128)S(1)} %get-tuple-element.15), channel_id=1, source_target_pairs={{0,16},{16,32},{32,48},{48,64},{64,80},{80,96},{96,112},{112,128},... | collective-permute-start | bytes 49160 | tf_op jit(solution)/shard_map/ppermute | solution.py:18
  38.8 15.0 %copy-start.2 = (f32[64,4096]{1,0:T(8,128)}, f32[64,4096]{1,0:T(8,128)S(1)}, u32[]{:S(2)}) copy-start(f32[64,4096]{1,0:T(8,128)S(1)} %fusion.24) | copy-start | bytes 3145732
  39.0 12.0 %collective-permute-start.10 = (f32[64,64]{1,0:T(8,128)S(1)}, f32[64,64]{1,0:T(8,128)S(1)}, u32[]{:S(2)}, u32[]{:S(2)}) collective-permute-start(f32[64,64]{1,0:T(8,128)S(1)} %get-tuple-element.12), channel_id=1, source_target_pairs={{1,0},{2,1},{3,2},{4,3},{5,4},{6,5},{7,6},{8,7},{9,8},{10,9},{11,1... | collective-permute-start | bytes 49160 | tf_op jit(solution)/shard_map/ppermute | solution.py:21
  40.3 10.7 %collective-permute-start.11 = (f32[64,64]{1,0:T(8,128)S(1)}, f32[64,64]{1,0:T(8,128)S(1)}, u32[]{:S(2)}, u32[]{:S(2)}) collective-permute-start(f32[64,64]{1,0:T(8,128)S(1)} %get-tuple-element.13), channel_id=1, source_target_pairs={{0,1},{1,2},{2,3},{3,4},{4,5},{5,6},{6,7},{7,8},{8,9},{9,10},{10,1... | collective-permute-start | bytes 49160 | tf_op jit(solution)/shard_map/ppermute | solution.py:18
  44.3 6.7 %collective-permute-start.8 = (f32[1,4096]{1,0:T(1,128)S(1)}, f32[1,4096]{1,0:T(1,128)S(1)}, u32[]{:S(2)}, u32[]{:S(2)}) collective-permute-start(f32[1,4096]{1,0:T(1,128)S(1)} %get-tuple-element.10), channel_id=1, source_target_pairs={{16,0},{32,16},{48,32},{64,48},{80,64},{96,80},{112,96},{128,112},... | collective-permute-start | bytes 49160 | tf_op jit(solution)/shard_map/ppermute | solution.py:21
  46.5 5.3 %collective-permute-start.9 = (f32[1,4096]{1,0:T(1,128)S(1)}, f32[1,4096]{1,0:T(1,128)S(1)}, u32[]{:S(2)}, u32[]{:S(2)}) collective-permute-start(f32[1,4096]{1,0:T(1,128)S(1)} %get-tuple-element.11), channel_id=1, source_target_pairs={{0,16},{16,32},{32,48},{48,64},{64,80},{80,96},{96,112},{112,128},... | collective-permute-start | bytes 49160 | tf_op jit(solution)/shard_map/ppermute | solution.py:18
  54.8 13.9 %collective-permute-start.14 = (f32[64,64]{1,0:T(8,128)S(1)}, f32[64,64]{1,0:T(8,128)S(1)}, u32[]{:S(2)}, u32[]{:S(2)}) collective-permute-start(f32[64,64]{1,0:T(8,128)S(1)} %get-tuple-element.8), channel_id=1, source_target_pairs={{1,0},{2,1},{3,2},{4,3},{5,4},{6,5},{7,6},{8,7},{9,8},{10,9},{11,1... | collective-permute-start | bytes 49160 | tf_op jit(solution)/shard_map/ppermute | solution.py:21
  56.1 12.6 %collective-permute-start.15 = (f32[64,64]{1,0:T(8,128)S(1)}, f32[64,64]{1,0:T(8,128)S(1)}, u32[]{:S(2)}, u32[]{:S(2)}) collective-permute-start(f32[64,64]{1,0:T(8,128)S(1)} %get-tuple-element.9), channel_id=1, source_target_pairs={{0,1},{1,2},{2,3},{3,4},{4,5},{5,6},{6,7},{7,8},{8,9},{9,10},{10,1... | collective-permute-start | bytes 49160 | tf_op jit(solution)/shard_map/ppermute | solution.py:18
  60.7 8.0 %collective-permute-start.12 = (f32[1,4096]{1,0:T(1,128)S(1)}, f32[1,4096]{1,0:T(1,128)S(1)}, u32[]{:S(2)}, u32[]{:S(2)}) collective-permute-start(f32[1,4096]{1,0:T(1,128)S(1)} %get-tuple-element.6), channel_id=1, source_target_pairs={{16,0},{32,16},{48,32},{64,48},{80,64},{96,80},{112,96},{128,112},... | collective-permute-start | bytes 49160 | tf_op jit(solution)/shard_map/ppermute | solution.py:21
  62.6 6.1 %collective-permute-start.13 = (f32[1,4096]{1,0:T(1,128)S(1)}, f32[1,4096]{1,0:T(1,128)S(1)}, u32[]{:S(2)}, u32[]{:S(2)}) collective-permute-start(f32[1,4096]{1,0:T(1,128)S(1)} %get-tuple-element.7), channel_id=1, source_target_pairs={{0,16},{16,32},{32,48},{48,64},{64,80},{80,96},{96,112},{112,128},... | collective-permute-start | bytes 49160 | tf_op jit(solution)/shard_map/ppermute | solution.py:18
  74.4 5.5 %copy-start.7 = (f32[256]{0:T(256)S(1)}, f32[256]{0:T(256)}, u32[]{:S(2)}) copy-start(f32[256]{0:T(256)} %param.8) | copy-start | bytes 3076
  74.4 184.7 %copy-start.4 = (f32[4096,64]{0,1:T(8,128)S(1)}, f32[4096,64]{0,1:T(8,128)}, u32[]{:S(2)}) copy-start(f32[4096,64]{0,1:T(8,128)} %copy.9) | copy-start | bytes 3145732
  (1 other events, 1.0 us)
where the time goes:
time: 267 us; the launch traced here: 266 us
  blocking collectives  164 us (61%)
  starting transfers between devices  48 us (18%)
  other arithmetic  25.1 us (9%)
  local copies, waits for them, and re-layouts  20.6 us (8%)
  matrix products  5.31 us (2%)
    psum x1, blocking collectives, per_device(): misfit_total = lax.psum(own_misfit, ('gx', 'gy'))  89.7 us
    psum x1, blocking collectives, per_device(): gram, cross = lax.psum((own_gram, own_cross), ('gx', 'gy'))  74.2 us
    ppermute x8, starting transfers between devices, padded(): lax.ppermute(lax.slice_in_dim(block, block.shape[dim] - width, None, axis...  30.6 us
    ppermute x8, starting transfers between devices, padded(): lax.ppermute(lax.slice_in_dim(block, 0, width, axis=dim), axis, backward)  17.4 us
    another operation x3, other arithmetic, per_device(): factor = jnp.linalg.cholesky(system)  6.55 us
    add x1, other arithmetic, chebyshev(): total = total + coeffs[order] * following  5.64 us
    another operation x2, other arithmetic, chol_solve(): lax.linalg.triangular_solve(factor, lower_sol, left_side=True, lower=True...  5.53 us
  transfers between devices with their start and end apart: 16, of which 2 were waited for; matrix products, arithmetic and copies ran while one was open for 4% of the time, Pallas kernels for 0%

commit v1 on v0

--- a/solution.py
+++ b/solution.py
@@ -90,7 +90,7 @@
         precision=lax.Precision.HIGHEST,
         preferred_element_type=jnp.float32,
     )
-    gram, cross = lax.psum((own_gram, own_cross), ("gx", "gy"))
+    gram, cross = lax.psum(lax.psum((own_gram, own_cross), "gy"), "gx")
     system = (MEMBERS - 1) * jnp.eye(MEMBERS, dtype=jnp.float32) + gram
     factor = jnp.linalg.cholesky(system)
     gain = chol_solve(factor, cross)

time: 267 us -> 307 us (1.15)
  blocking collectives: 164 us -> 204 us
    psum x1 -> x2, blocking collectives: 74.2 us -> 114 us  [per_device(): gram, cross = lax.psum(lax.psum((own_gram, own_cross), 'gy'), 'gx')]
  transfers between devices with their start and end apart: 16 -> 16, of which waited for: 2 -> 2; matrix products, arithmetic and copies ran while one was open for 4% -> 3% of each run, Pallas kernels for 0% -> 0%
where the time goes in v1:
time: 307 us; the launch traced here: 306 us
  blocking collectives  204 us (66%)
  starting transfers between devices  48 us (16%)
  other arithmetic  25 us (8%)
  local copies, waits for them, and re-layouts  20.6 us (7%)
  matrix products  5.31 us (2%)
    psum x2, blocking collectives, per_device(): gram, cross = lax.psum(lax.psum((own_gram, own_cross), 'gy'), 'gx')  114 us
    psum x1, blocking collectives, per_device(): misfit_total = lax.psum(own_misfit, ('gx', 'gy'))  89.7 us
    ppermute x8, starting transfers between devices, padded(): lax.ppermute(lax.slice_in_dim(block, block.shape[dim] - width, None, axis...  30.6 us
    ppermute x8, starting transfers between devices, padded(): lax.ppermute(lax.slice_in_dim(block, 0, width, axis=dim), axis, backward)  17.4 us
    another operation x3, other arithmetic, per_device(): factor = jnp.linalg.cholesky(system)  6.54 us
  transfers between devices with their start and end apart: 16, of which 2 were waited for; matrix products, arithmetic and copies ran while one was open for 3% of the time, Pallas kernels for 0%

profile of v1, /device:TPU:1, one launch (start us, length us, event | category | flops | bytes accessed | tf_op | source)
XLA Modules:
  0.0 305.9 jit_solution(369535335735685167)
XLA Ops:
  2.8 4.6 %collective-permute-start.3 = (f32[64,64]{1,0:T(8,128)S(1)}, f32[64,64]{1,0:T(8,128)S(1)}, u32[]{:S(2)}, u32[]{:S(2)}) collective-permute-start(f32[64,64]{1,0:T(8,128)S(1)} %get-tuple-element.23), channel_id=1, source_target_pairs={{0,1},{1,2},{2,3},{3,4},{4,5},{5,6},{6,7},{7,8},{8,9},{9,10},{10,1... | collective-permute-start | bytes 49160 | tf_op jit(solution)/shard_map/ppermute | solution.py:18
  8.4 5.1 %collective-permute-start = (f32[1,4096]{1,0:T(1,128)S(1)}, f32[1,4096]{1,0:T(1,128)S(1)}, u32[]{:S(2)}, u32[]{:S(2)}) collective-permute-start(f32[1,4096]{1,0:T(1,128)S(1)} %get-tuple-element.20), channel_id=1, source_target_pairs={{16,0},{32,16},{48,32},{64,48},{80,64},{96,80},{112,96},{128,112},... | collective-permute-start | bytes 49160 | tf_op jit(solution)/shard_map/ppermute | solution.py:21
  15.4 2.0 reshape.43
  18.1 1.9 broadcast_in_dim.23
  20.1 3.0 reshape.44
  26.4 4.0 %collective-permute-start.7 = (f32[64,64]{1,0:T(8,128)S(1)}, f32[64,64]{1,0:T(8,128)S(1)}, u32[]{:S(2)}, u32[]{:S(2)}) collective-permute-start(f32[64,64]{1,0:T(8,128)S(1)} %get-tuple-element.19), channel_id=1, source_target_pairs={{0,1},{1,2},{2,3},{3,4},{4,5},{5,6},{6,7},{7,8},{8,9},{9,10},{10,1... | collective-permute-start | bytes 49160 | tf_op jit(solution)/shard_map/ppermute | solution.py:18
  30.4 3.0 collective-permute-start.4
  33.4 2.6 collective-permute-start.5
  36.8 2.0 fusion.24
  40.2 4.0 %collective-permute-start.11 = (f32[64,64]{1,0:T(8,128)S(1)}, f32[64,64]{1,0:T(8,128)S(1)}, u32[]{:S(2)}, u32[]{:S(2)}) collective-permute-start(f32[64,64]{1,0:T(8,128)S(1)} %get-tuple-element.15), channel_id=1, source_target_pairs={{0,1},{1,2},{2,3},{3,4},{4,5},{5,6},{6,7},{7,8},{8,9},{9,10},{10,1... | collective-permute-start | bytes 49160 | tf_op jit(solution)/shard_map/ppermute | solution.py:18
  44.2 2.3 collective-permute-start.8
  46.5 4.4 %collective-permute-start.9 = (f32[1,4096]{1,0:T(1,128)S(1)}, f32[1,4096]{1,0:T(1,128)S(1)}, u32[]{:S(2)}, u32[]{:S(2)}) collective-permute-start(f32[1,4096]{1,0:T(1,128)S(1)} %get-tuple-element.13), channel_id=1, source_target_pairs={{0,16},{16,32},{32,48},{48,64},{64,80},{80,96},{96,112},{112,128},... | collective-permute-start | bytes 49160 | tf_op jit(solution)/shard_map/ppermute | solution.py:18
  51.8 2.0 fusion.16
  56.1 4.6 %collective-permute-start.15 = (f32[64,64]{1,0:T(8,128)S(1)}, f32[64,64]{1,0:T(8,128)S(1)}, u32[]{:S(2)}, u32[]{:S(2)}) collective-permute-start(f32[64,64]{1,0:T(8,128)S(1)} %get-tuple-element.11), channel_id=1, source_target_pairs={{0,1},{1,2},{2,3},{3,4},{4,5},{5,6},{6,7},{7,8},{8,9},{9,10},{10,1... | collective-permute-start | bytes 49160 | tf_op jit(solution)/shard_map/ppermute | solution.py:18
  62.6 4.5 %collective-permute-start.13 = (f32[1,4096]{1,0:T(1,128)S(1)}, f32[1,4096]{1,0:T(1,128)S(1)}, u32[]{:S(2)}, u32[]{:S(2)}) collective-permute-start(f32[1,4096]{1,0:T(1,128)S(1)} %get-tuple-element.9), channel_id=1, source_target_pairs={{0,16},{16,32},{32,48},{48,64},{64,80},{80,96},{96,112},{112,128},... | collective-permute-start | bytes 49160 | tf_op jit(solution)/shard_map/ppermute | solution.py:18
  68.7 5.5 %fusion.8 = f32[64,4096]{1,0:T(8,128)} fusion(f32[64,4096]{1,0:T(8,128)} %copy-done.2, f32[64,4096]{1,0:T(8,128)} %copy-done.3, f32[64,64]{1,0:T(8,128)S(1)} %collective-permute-done.15, f32[64,64]{1,0:T(8,128)S(1)} %collective-permute-done.14, f32[1,4096]{1,0:T(1,128)S(1)} %collective-permute-done.13, f32[1,4096]{1,0:T(1,128)S(1)} %collective-permute-done.12, ...), kind=kLoop, calls=%fused_computation.11 | loop fusion | flops 9175040 | bytes 5373952 | tf_op jit(solution)/shard_map/add | solution.py:57
  74.3 3.2 %reshape.45 = f32[4096,64]{1,0:T(8,128)} reshape(f32[64,4096]{1,0:T(8,128)} %fusion.8) | data formatting | bytes 2097152 | tf_op jit(solution)/shard_map/reshape | solution.py:74
  77.5 2.3 gather_fusion
  80.6 89.7 %psum.35 = f32[]{:T(128)} all-reduce(f32[]{:T(128)} %get-tuple-element.3), channel_id=1, replica_groups=mesh['gx'=16,'gy'=16] {'gx','gy'}, use_global_device_ids=true, to_apply=%region_3.4 | all-reduce | flops 1 | bytes 8 | tf_op jit(solution)/shard_map/psum | solution.py:81
  172.1 57.0 %all-reduce = (f32[64,64]{1,0:T(8,128)S(1)}, f32[64,64]{1,0:T(8,128)S(1)}) all-reduce(f32[64,64]{1,0:T(8,128)S(1)} %fusion.34, f32[64,64]{1,0:T(8,128)S(1)} %fusion.36), channel_id=1, replica_groups=mesh['gx'=16,'gy'=16] {'gy'}, use_global_device_ids=true, to_apply=%region_8.9 | all-reduce | flops 8192 | bytes 65536 | tf_op jit(solution)/shard_map/psum | solution.py:93
  229.1 57.0 %all-reduce.1 = (f32[64,64]{1,0:T(8,128)S(1)}, f32[64,64]{1,0:T(8,128)S(1)}) all-reduce(f32[64,64]{1,0:T(8,128)S(1)} %get-tuple-element.4, f32[64,64]{1,0:T(8,128)S(1)} %get-tuple-element.5), channel_id=1, replica_groups=mesh['gx'=16,'gy'=16] {'gx'}, use_global_device_ids=true, to_apply=%region_9.10 | all-reduce | flops 8192 | bytes 65536 | tf_op jit(solution)/shard_map/psum | solution.py:93
  286.2 5.8 %cholesky.16 = f32[64,64]{1,0:T(8,128)S(1)} custom-call(f32[64,64]{1,0:T(8,128)S(1)} %fusion.57), custom_call_target="Cholesky" | custom-call | tf_op jit(solution)/shard_map/jit(cholesky)/cholesky | solution.py:95
  293.4 4.9 %custom-call.8 = f32[1,64,64]{1,2,0:T(8,128)S(1)} custom-call(f32[1,64,64]{2,1,0:T(8,128)S(1)} %fusion.52), custom_call_target="InvertDiagBlocksLowerTriangular" | custom-call | tf_op jit(solution)/shard_map/triangular_solve | solution.py:40
  298.8 3.7 %convolution_add_fusion = f32[4096,64]{0,1:T(8,128)} fusion(f32[4096,64]{0,1:T(8,128)S(1)} %copy-done.4, f32[64,64]{1,0:T(8,128)S(1)} %fusion.53, f32[4096,64]{1,0:T(8,128)S(1)} %reshape.43, f32[4096]{0:T(1024)S(1)} %broadcast_multiply_fusion.1), kind=kOutput, calls=%fused_computation.1 | convolution fusion | flops 201850880 | bytes 3178496 | tf_op jit(solution)/shard_map/dot_general | solution.py:99
  (72 shorter events, 25.1 us)
Async XLA Ops:
  0.6 16.8 %copy-start.5 = (f32[64,64]{1,0:T(8,128)S(1)}, f32[64,64]{1,0:T(8,128)}, u32[]{:S(2)}) copy-start(f32[64,64]{1,0:T(8,128)} %param.6) | copy-start | bytes 49156
  1.5 21.5 %collective-permute-start.2 = (f32[64,64]{1,0:T(8,128)S(1)}, f32[64,64]{1,0:T(8,128)S(1)}, u32[]{:S(2)}, u32[]{:S(2)}) collective-permute-start(f32[64,64]{1,0:T(8,128)S(1)} %get-tuple-element.22), channel_id=1, source_target_pairs={{1,0},{2,1},{3,2},{4,3},{5,4},{6,5},{7,6},{8,7},{9,8},{10,9},{11,1... | collective-permute-start | bytes 49160 | tf_op jit(solution)/shard_map/ppermute | solution.py:21
  2.8 20.3 %collective-permute-start.3 = (f32[64,64]{1,0:T(8,128)S(1)}, f32[64,64]{1,0:T(8,128)S(1)}, u32[]{:S(2)}, u32[]{:S(2)}) collective-permute-start(f32[64,64]{1,0:T(8,128)S(1)} %get-tuple-element.23), channel_id=1, source_target_pairs={{0,1},{1,2},{2,3},{3,4},{4,5},{5,6},{6,7},{7,8},{8,9},{9,10},{10,1... | collective-permute-start | bytes 49160 | tf_op jit(solution)/shard_map/ppermute | solution.py:18
  8.4 14.7 %collective-permute-start = (f32[1,4096]{1,0:T(1,128)S(1)}, f32[1,4096]{1,0:T(1,128)S(1)}, u32[]{:S(2)}, u32[]{:S(2)}) collective-permute-start(f32[1,4096]{1,0:T(1,128)S(1)} %get-tuple-element.20), channel_id=1, source_target_pairs={{16,0},{32,16},{48,32},{64,48},{80,64},{96,80},{112,96},{128,112},... | collective-permute-start | bytes 49160 | tf_op jit(solution)/shard_map/ppermute | solution.py:21
  13.5 4.6 %copy-start.8 = (s32[256]{0:T(256)S(1)}, s32[256]{0:T(256)}, u32[]{:S(2)}) copy-start(s32[256]{0:T(256)} %param.7) | copy-start | bytes 3076
  13.5 9.6 %collective-permute-start.1 = (f32[1,4096]{1,0:T(1,128)S(1)}, f32[1,4096]{1,0:T(1,128)S(1)}, u32[]{:S(2)}, u32[]{:S(2)}) collective-permute-start(f32[1,4096]{1,0:T(1,128)S(1)} %get-tuple-element.21), channel_id=1, source_target_pairs={{0,16},{16,32},{32,48},{48,64},{64,80},{80,96},{96,112},{112,128},... | collective-permute-start | bytes 49160 | tf_op jit(solution)/shard_map/ppermute | solution.py:18
  20.1 3.0 copy-start
  23.0 13.0 %copy-start.6 = (f32[256]{0:T(256)S(1)}, f32[256]{0:T(256)}, u32[]{:S(2)}) copy-start(f32[256]{0:T(256)} %param.9) | copy-start | bytes 3076
  23.0 13.8 %copy-start.1 = (f32[64,4096]{1,0:T(8,128)S(1)}, f32[64,4096]{1,0:T(8,128)}, u32[]{:S(2)}) copy-start(f32[64,4096]{1,0:T(8,128)} %reshape.44) | copy-start | bytes 3145732
  25.1 10.9 %collective-permute-start.6 = (f32[64,64]{1,0:T(8,128)S(1)}, f32[64,64]{1,0:T(8,128)S(1)}, u32[]{:S(2)}, u32[]{:S(2)}) collective-permute-start(f32[64,64]{1,0:T(8,128)S(1)} %get-tuple-element.18), channel_id=1, source_target_pairs={{1,0},{2,1},{3,2},{4,3},{5,4},{6,5},{7,6},{8,7},{9,8},{10,9},{11,1... | collective-permute-start | bytes 49160 | tf_op jit(solution)/shard_map/ppermute | solution.py:21
  26.4 9.6 %collective-permute-start.7 = (f32[64,64]{1,0:T(8,128)S(1)}, f32[64,64]{1,0:T(8,128)S(1)}, u32[]{:S(2)}, u32[]{:S(2)}) collective-permute-start(f32[64,64]{1,0:T(8,128)S(1)} %get-tuple-element.19), channel_id=1, source_target_pairs={{0,1},{1,2},{2,3},{3,4},{4,5},{5,6},{6,7},{7,8},{8,9},{9,10},{10,1... | collective-permute-start | bytes 49160 | tf_op jit(solution)/shard_map/ppermute | solution.py:18
  30.4 5.6 %collective-permute-start.4 = (f32[1,4096]{1,0:T(1,128)S(1)}, f32[1,4096]{1,0:T(1,128)S(1)}, u32[]{:S(2)}, u32[]{:S(2)}) collective-permute-start(f32[1,4096]{1,0:T(1,128)S(1)} %get-tuple-element.16), channel_id=1, source_target_pairs={{16,0},{32,16},{48,32},{64,48},{80,64},{96,80},{112,96},{128,112},... | collective-permute-start | bytes 49160 | tf_op jit(solution)/shard_map/ppermute | solution.py:21
  33.4 3.5 %collective-permute-start.5 = (f32[1,4096]{1,0:T(1,128)S(1)}, f32[1,4096]{1,0:T(1,128)S(1)}, u32[]{:S(2)}, u32[]{:S(2)}) collective-permute-start(f32[1,4096]{1,0:T(1,128)S(1)} %get-tuple-element.17), channel_id=1, source_target_pairs={{0,16},{16,32},{32,48},{48,64},{64,80},{80,96},{96,112},{112,128},... | collective-permute-start | bytes 49160 | tf_op jit(solution)/shard_map/ppermute | solution.py:18
  38.8 15.0 %copy-start.2 = (f32[64,4096]{1,0:T(8,128)}, f32[64,4096]{1,0:T(8,128)S(1)}, u32[]{:S(2)}) copy-start(f32[64,4096]{1,0:T(8,128)S(1)} %fusion.24) | copy-start | bytes 3145732
  38.9 12.0 %collective-permute-start.10 = (f32[64,64]{1,0:T(8,128)S(1)}, f32[64,64]{1,0:T(8,128)S(1)}, u32[]{:S(2)}, u32[]{:S(2)}) collective-permute-start(f32[64,64]{1,0:T(8,128)S(1)} %get-tuple-element.14), channel_id=1, source_target_pairs={{1,0},{2,1},{3,2},{4,3},{5,4},{6,5},{7,6},{8,7},{9,8},{10,9},{11,1... | collective-permute-start | bytes 49160 | tf_op jit(solution)/shard_map/ppermute | solution.py:21
  40.2 10.7 %collective-permute-start.11 = (f32[64,64]{1,0:T(8,128)S(1)}, f32[64,64]{1,0:T(8,128)S(1)}, u32[]{:S(2)}, u32[]{:S(2)}) collective-permute-start(f32[64,64]{1,0:T(8,128)S(1)} %get-tuple-element.15), channel_id=1, source_target_pairs={{0,1},{1,2},{2,3},{3,4},{4,5},{5,6},{6,7},{7,8},{8,9},{9,10},{10,1... | collective-permute-start | bytes 49160 | tf_op jit(solution)/shard_map/ppermute | solution.py:18
  44.2 6.7 %collective-permute-start.8 = (f32[1,4096]{1,0:T(1,128)S(1)}, f32[1,4096]{1,0:T(1,128)S(1)}, u32[]{:S(2)}, u32[]{:S(2)}) collective-permute-start(f32[1,4096]{1,0:T(1,128)S(1)} %get-tuple-element.12), channel_id=1, source_target_pairs={{16,0},{32,16},{48,32},{64,48},{80,64},{96,80},{112,96},{128,112},... | collective-permute-start | bytes 49160 | tf_op jit(solution)/shard_map/ppermute | solution.py:21
  46.5 5.3 %collective-permute-start.9 = (f32[1,4096]{1,0:T(1,128)S(1)}, f32[1,4096]{1,0:T(1,128)S(1)}, u32[]{:S(2)}, u32[]{:S(2)}) collective-permute-start(f32[1,4096]{1,0:T(1,128)S(1)} %get-tuple-element.13), channel_id=1, source_target_pairs={{0,16},{16,32},{32,48},{48,64},{64,80},{80,96},{96,112},{112,128},... | collective-permute-start | bytes 49160 | tf_op jit(solution)/shard_map/ppermute | solution.py:18
  54.8 13.9 %collective-permute-start.14 = (f32[64,64]{1,0:T(8,128)S(1)}, f32[64,64]{1,0:T(8,128)S(1)}, u32[]{:S(2)}, u32[]{:S(2)}) collective-permute-start(f32[64,64]{1,0:T(8,128)S(1)} %get-tuple-element.10), channel_id=1, source_target_pairs={{1,0},{2,1},{3,2},{4,3},{5,4},{6,5},{7,6},{8,7},{9,8},{10,9},{11,1... | collective-permute-start | bytes 49160 | tf_op jit(solution)/shard_map/ppermute | solution.py:21
  56.1 12.6 %collective-permute-start.15 = (f32[64,64]{1,0:T(8,128)S(1)}, f32[64,64]{1,0:T(8,128)S(1)}, u32[]{:S(2)}, u32[]{:S(2)}) collective-permute-start(f32[64,64]{1,0:T(8,128)S(1)} %get-tuple-element.11), channel_id=1, source_target_pairs={{0,1},{1,2},{2,3},{3,4},{4,5},{5,6},{6,7},{7,8},{8,9},{9,10},{10,1... | collective-permute-start | bytes 49160 | tf_op jit(solution)/shard_map/ppermute | solution.py:18
  60.7 8.0 %collective-permute-start.12 = (f32[1,4096]{1,0:T(1,128)S(1)}, f32[1,4096]{1,0:T(1,128)S(1)}, u32[]{:S(2)}, u32[]{:S(2)}) collective-permute-start(f32[1,4096]{1,0:T(1,128)S(1)} %get-tuple-element.8), channel_id=1, source_target_pairs={{16,0},{32,16},{48,32},{64,48},{80,64},{96,80},{112,96},{128,112},... | collective-permute-start | bytes 49160 | tf_op jit(solution)/shard_map/ppermute | solution.py:21
  62.6 6.1 %collective-permute-start.13 = (f32[1,4096]{1,0:T(1,128)S(1)}, f32[1,4096]{1,0:T(1,128)S(1)}, u32[]{:S(2)}, u32[]{:S(2)}) collective-permute-start(f32[1,4096]{1,0:T(1,128)S(1)} %get-tuple-element.9), channel_id=1, source_target_pairs={{0,16},{16,32},{32,48},{48,64},{64,80},{80,96},{96,112},{112,128},... | collective-permute-start | bytes 49160 | tf_op jit(solution)/shard_map/ppermute | solution.py:18
  74.3 5.5 %copy-start.7 = (f32[256]{0:T(256)S(1)}, f32[256]{0:T(256)}, u32[]{:S(2)}) copy-start(f32[256]{0:T(256)} %param.8) | copy-start | bytes 3076
  74.3 224.5 %copy-start.4 = (f32[4096,64]{0,1:T(8,128)S(1)}, f32[4096,64]{0,1:T(8,128)}, u32[]{:S(2)}) copy-start(f32[4096,64]{0,1:T(8,128)} %copy.9) | copy-start | bytes 3145732
  (1 other events, 1.0 us)
